TPU v7x, 32 devices: a whole 2x2x4 slice. The times are simulated.
32 devices in a mesh: groups: 2 (over y), seq: 4 (over z), heads: 4 (over x, core).
Axes of the slice: x: 2, y: 2, z: 4, core: 2. Of those that a mesh axis runs over, the one named last changes fastest.
Arguments:
- queries: bfloat16 [4096, 24, 128], P(('groups', 'seq'), 'heads'), parts along dimension 0, may hold values from -130 to 130
- keys: bfloat16 [4096, 24, 128], P(('groups', 'seq'), 'heads'), parts along dimension 0, may hold values from -6 to 6
- values: bfloat16 [4096, 24, 128], P(('groups', 'seq'), 'heads'), parts along dimension 0, may hold values from -6 to 6
- pool_keys: bfloat16 [24, 8, 128], P('heads'), may hold values from -0.5 to 0.5
- pool_values: bfloat16 [24, 8, 128], P('heads'), may hold values from -0.5 to 0.5
Outputs:
- attended: bfloat16 [4096, 24, 128], P(('groups', 'seq'), 'heads'), parts along dimension 0
There are 2 independent parts, one for each index of `groups`. A program takes and returns all parts, laid end to end along the dimension named above; an argument that names none is the same for every part. Nothing has to cross between parts.
All inputs are finite; a program needn't handle non-finite values.
Results may differ from a plain program's by a relative error of at most 0.01.
Values may be sent and summed in bfloat16 or wider, within the bound.
A program may use at most 64 MiB of HBM per device.

v0:
```python
import functools
import math

import jax
import jax.numpy as jnp
from jax import lax
from jax.experimental import pallas as pl
from jax.experimental.pallas import tpu as pltpu
from jax.sharding import PartitionSpec as P

NEG = -1e30
F32 = jnp.float32
BF16 = jnp.bfloat16


def dot_t(a, b):
    return lax.dot_general(a, b, (((1,), (1,)), ((), ())), preferred_element_type=F32)


def dot(a, b):
    return jnp.dot(a, b, preferred_element_type=F32)


def kernel(
    peers, q_hbm, k_hbm, v_hbm, pk_ref, pv_ref, o_hbm,
    q_buf, k_buf, v_buf, o_buf, prev, summ, top_s, total_s, acc_s,
    in_sem, out_sem, prev_send, prev_recv, sum_send, sum_recv,
):
    heads, rows, width = q_buf.shape
    sums, block = pk_ref.shape[1], pk_ref.shape[2]
    blocks = rows // block
    own = blocks * sums
    gain = (width ** -0.5) * math.log2(math.e)
    spot = lax.axis_index("seq")

    k_in = pltpu.make_async_copy(k_hbm, k_buf, in_sem.at[0])
    v_in = pltpu.make_async_copy(v_hbm, v_buf, in_sem.at[1])
    q_in = pltpu.make_async_copy(q_hbm, q_buf, in_sem.at[2])
    k_in.start()
    v_in.start()
    q_in.start()

    barrier = pltpu.get_barrier_semaphore()

    def greet(i, c):
        pl.semaphore_signal(
            barrier, inc=1, device_id={"seq": i}, device_id_type=pl.DeviceIdType.MESH
        )
        return c

    lax.fori_loop(0, spot, greet, 0)

    def clear(i, c):
        summ[i] = jnp.zeros(summ.shape[1:], BF16)
        return c

    lax.fori_loop(spot + 1, summ.shape[0], clear, 0)

    @pl.when(spot == 0)
    def _():
        prev[...] = jnp.zeros(prev.shape, BF16)

    @pl.when(spot < peers - 1)
    def _():
        pl.semaphore_wait(barrier, peers - 1 - spot)

    def prev_copy(i, ref, to):
        return pltpu.make_async_remote_copy(
            src_ref=ref.at[:, pl.ds(rows - block, block), :],
            dst_ref=prev.at[i],
            send_sem=prev_send.at[i],
            recv_sem=prev_recv.at[i],
            device_id={"seq": to},
            device_id_type=pl.DeviceIdType.MESH,
        )

    @pl.when(spot < peers - 1)
    def _():
        prev_copy(0, k_hbm, spot + 1).start()
        prev_copy(1, v_hbm, spot + 1).start()

    row_group = lax.broadcasted_iota(jnp.int32, (own, block), 0) // sums

    def summarise(which, pool_ref, buf, h):
        pool = pool_ref[h].astype(F32)
        tall = jnp.concatenate([pool] * blocks, axis=0)
        wide = jnp.concatenate(
            [jnp.where(row_group == b, tall, 0.0) for b in range(blocks)], axis=1
        ).astype(BF16)
        summ[spot, which, h] = dot(wide, buf[h]).astype(BF16)

    k_in.wait()
    for h in range(heads):
        summarise(0, pk_ref, k_buf, h)
    v_in.wait()
    for h in range(heads):
        summarise(1, pv_ref, v_buf, h)

    def sum_copy(source, to):
        return pltpu.make_async_remote_copy(
            src_ref=summ.at[source],
            dst_ref=summ.at[source],
            send_sem=sum_send.at[to],
            recv_sem=sum_recv.at[source],
            device_id={"seq": to},
            device_id_type=pl.DeviceIdType.MESH,
        )

    def send(i, c):
        sum_copy(spot, i).start()
        return c

    lax.fori_loop(spot + 1, peers, send, 0)
    q_in.wait()

    r = lax.broadcasted_iota(jnp.int32, (block, block), 0)
    c = lax.broadcasted_iota(jnp.int32, (block, block), 1)
    lower = c <= r

    def window(scores, v_now, v_before):
        top = jnp.max(scores, axis=1, keepdims=True)
        weights = jnp.exp2((scores - top) * gain)
        total = jnp.sum(weights, axis=1, keepdims=True)
        near = jnp.where(lower, weights, 0.0).astype(BF16)
        far = jnp.where(lower, 0.0, weights).astype(BF16)
        return top, total, dot(near, v_now) + dot(far, v_before)

    def keep(h, b, top, total, acc):
        at = pl.ds(b * block, block)
        top_s[h, at, :] = jnp.broadcast_to(top, (block, width))
        total_s[h, at, :] = jnp.broadcast_to(total, (block, width))
        acc_s[h, at, :] = acc

    def near_head(h, carry):
        for b in range(1, blocks):
            now, before = pl.ds(b * block, block), pl.ds((b - 1) * block, block)
            q = q_buf[h, now, :]
            scores = jnp.where(lower, dot_t(q, k_buf[h, now, :]), dot_t(q, k_buf[h, before, :]))
            keep(h, b, *window(scores, v_buf[h, now, :], v_buf[h, before, :]))
        return carry

    lax.fori_loop(0, heads, near_head, 0)

    @pl.when(spot > 0)
    def _():
        prev_copy(0, k_hbm, spot).wait_recv()
        prev_copy(1, v_hbm, spot).wait_recv()

    def land(i, c):
        sum_copy(i, spot).wait_recv()
        return c

    lax.fori_loop(0, spot, land, 0)

    per = block // own
    seen = (lower | (spot > 0))

    def o_copy(h):
        return pltpu.make_async_copy(o_buf.at[h], o_hbm.at[h], out_sem.at[h])

    def far_head(h, carry):
        now = pl.ds(0, block)
        q = q_buf[h, now, :]
        scores = jnp.where(lower, dot_t(q, k_buf[h, now, :]), dot_t(q, prev[0, h]))
        scores = jnp.where(seen, scores, NEG)
        keep(h, 0, *window(scores, v_buf[h, now, :], prev[1, h]))

        def chunk(j, carry):
            keys = jnp.concatenate([summ[j * per + i, 0, h] for i in range(per)], axis=0)
            values = jnp.concatenate([summ[j * per + i, 1, h] for i in range(per)], axis=0)
            for b in range(blocks):
                at = pl.ds(b * block, block)
                row_block = j * (block // sums) + c // sums
                scores = dot_t(q_buf[h, at, :], keys)
                scores = jnp.where(row_block < spot * blocks + b, scores, NEG)
                old = top_s[h, at, :]
                top = jnp.maximum(old, jnp.max(scores, axis=1, keepdims=True))
                weights = jnp.exp2((scores - top) * gain)
                fade = jnp.exp2((old - top) * gain)
                top_s[h, at, :] = top
                total_s[h, at, :] = total_s[h, at, :] * fade + jnp.sum(
                    weights, axis=1, keepdims=True
                )
                acc_s[h, at, :] = acc_s[h, at, :] * fade + dot(weights.astype(BF16), values)
            return carry

        chunks = summ.shape[0] // per
        if chunks == 1:
            chunk(0, 0)
        else:
            lax.fori_loop(0, (spot * own + own - sums + block - 1) // block, chunk, 0)
        o_buf[h] = (acc_s[h] / total_s[h]).astype(BF16)
        o_copy(h).start()
        return carry

    lax.fori_loop(0, heads, far_head, 0)

    @pl.when(spot < peers - 1)
    def _():
        prev_copy(0, k_hbm, spot + 1).wait_send()
        prev_copy(1, v_hbm, spot + 1).wait_send()

    def sent(i, c):
        sum_copy(spot, i).wait_send()
        return c

    lax.fori_loop(spot + 1, peers, sent, 0)
    for h in range(heads):
        o_copy(h).wait()


def on_device(peers, queries, keys, values, pool_keys, pool_values):
    rows, heads, width = queries.shape
    sums, block = pool_keys.shape[1], pool_keys.shape[2]
    own = rows // block * sums
    per = block // own
    slots = -(-peers // per) * per
    q, k, v = (jnp.moveaxis(x, 1, 0) for x in (queries, keys, values))
    hbm = pl.BlockSpec(memory_space=pl.ANY)
    vmem = pl.BlockSpec(memory_space=pltpu.VMEM)
    out = pl.pallas_call(
        functools.partial(kernel, peers),
        out_shape=jax.ShapeDtypeStruct((heads, rows, width), BF16),
        in_specs=[hbm, hbm, hbm, vmem, vmem],
        out_specs=hbm,
        scratch_shapes=[
            pltpu.VMEM((heads, rows, width), BF16),
            pltpu.VMEM((heads, rows, width), BF16),
            pltpu.VMEM((heads, rows, width), BF16),
            pltpu.VMEM((heads, rows, width), BF16),
            pltpu.VMEM((2, heads, block, width), BF16),
            pltpu.VMEM((slots, 2, heads, own, width), BF16),
            pltpu.VMEM((heads, rows, width), F32),
            pltpu.VMEM((heads, rows, width), F32),
            pltpu.VMEM((heads, rows, width), F32),
            pltpu.SemaphoreType.DMA((3,)),
            pltpu.SemaphoreType.DMA((heads,)),
            pltpu.SemaphoreType.DMA((2,)),
            pltpu.SemaphoreType.DMA((2,)),
            pltpu.SemaphoreType.DMA((peers,)),
            pltpu.SemaphoreType.DMA((peers,)),
        ],
        compiler_params=pltpu.CompilerParams(
            collective_id=0, has_side_effects=True, vmem_limit_bytes=40 * 1024 * 1024
        ),
    )(q, k, v, pool_keys, pool_values)
    return jnp.moveaxis(out, 0, 1)


def solution(mesh):
    in_specs = (
        P(("groups", "seq"), "heads", None),
        P(("groups", "seq"), "heads", None),
        P(("groups", "seq"), "heads", None),
        P("heads", None, None),
        P("heads", None, None),
    )
    out_specs = P(("groups", "seq"), "heads", None)
    return jax.shard_map(
        functools.partial(on_device, mesh.shape["seq"]),
        mesh=mesh, in_specs=in_specs, out_specs=out_specs, check_vma=False,
    )
```

profile of v0, /device:TPU:26, one launch (start us, length us, event | category | flops | bytes accessed | tf_op | source)
XLA Modules:
  0.0 32.8 jit_solution(7666896160599020650)
XLA Ops:
  0.0 0.0 copy-start
  0.0 1.1 %copy-done = bf16[512,6,128]{2,0,1:T(8,128)(2,1)S(1)} copy-done((bf16[512,6,128]{2,0,1:T(8,128)(2,1)S(1)}, bf16[512,6,128]{2,0,1:T(8,128)(2,1)}, u32[]{:S(2)}) %copy-start) | copy-done | bytes 786456
  1.1 0.0 copy-start.1
  1.1 1.1 %copy-done.1 = bf16[512,6,128]{2,0,1:T(8,128)(2,1)S(1)} copy-done((bf16[512,6,128]{2,0,1:T(8,128)(2,1)S(1)}, bf16[512,6,128]{2,0,1:T(8,128)(2,1)}, u32[]{:S(2)}) %copy-start.1) | copy-done | bytes 786456
  2.3 0.0 copy-start.2
  2.3 1.1 %copy-done.2 = bf16[512,6,128]{2,0,1:T(8,128)(2,1)S(1)} copy-done((bf16[512,6,128]{2,0,1:T(8,128)(2,1)S(1)}, bf16[512,6,128]{2,0,1:T(8,128)(2,1)}, u32[]{:S(2)}) %copy-start.2) | copy-done | bytes 786456
  3.4 0.0 copy-start.3
  3.4 0.7 %copy-done.3 = bf16[6,8,128]{2,1,0:T(8,128)(2,1)S(1)} copy-done((bf16[6,8,128]{2,1,0:T(8,128)(2,1)S(1)}, bf16[6,8,128]{2,1,0:T(8,128)(2,1)}, u32[]{:S(2)}) %copy-start.3) | copy-done | bytes 12312
  4.1 0.0 copy-start.4
  4.1 0.7 %copy-done.4 = bf16[6,8,128]{2,1,0:T(8,128)(2,1)S(1)} copy-done((bf16[6,8,128]{2,1,0:T(8,128)(2,1)S(1)}, bf16[6,8,128]{2,1,0:T(8,128)(2,1)}, u32[]{:S(2)}) %copy-start.4) | copy-done | bytes 12312
  4.8 27.1 %shard_map.55 = bf16[6,512,128]{2,1,0:T(8,128)(2,1)S(1)} custom-call(bf16[6,512,128]{2,1,0:T(8,128)(2,1)S(1)} %bitcast.5, bf16[6,512,128]{2,1,0:T(8,128)(2,1)S(1)} %bitcast.6, bf16[6,512,128]{2,1,0:T(8,128)(2,1)S(1)} %bitcast.7, bf16[6,8,128]{2,1,0:T(8,128)(2,1)S(1)} %copy-done.3, bf16[6,8,128]{2,1,0:T(8,128)(2,1)S(1)} %copy-done.4), custom_call_target="tpu_custom_call" | custom-call | tf_op jit(solution)/shard_map/pallas_call | solution.py:221
  32.0 0.9 %copy.7 = bf16[512,6,128]{2,0,1:T(8,128)(2,1)} copy(bf16[512,6,128]{2,0,1:T(8,128)(2,1)S(1)} %bitcast.4) | data formatting | bytes 1572864
Async XLA Ops:
  0.0 1.1 %copy-start = (bf16[512,6,128]{2,0,1:T(8,128)(2,1)S(1)}, bf16[512,6,128]{2,0,1:T(8,128)(2,1)}, u32[]{:S(2)}) copy-start(bf16[512,6,128]{2,0,1:T(8,128)(2,1)} %param.5) | copy-start | bytes 2359300
  1.1 1.1 %copy-start.1 = (bf16[512,6,128]{2,0,1:T(8,128)(2,1)S(1)}, bf16[512,6,128]{2,0,1:T(8,128)(2,1)}, u32[]{:S(2)}) copy-start(bf16[512,6,128]{2,0,1:T(8,128)(2,1)} %param.6) | copy-start | bytes 2359300
  2.3 1.1 %copy-start.2 = (bf16[512,6,128]{2,0,1:T(8,128)(2,1)S(1)}, bf16[512,6,128]{2,0,1:T(8,128)(2,1)}, u32[]{:S(2)}) copy-start(bf16[512,6,128]{2,0,1:T(8,128)(2,1)} %param.7) | copy-start | bytes 2359300
  3.4 0.7 %copy-start.3 = (bf16[6,8,128]{2,1,0:T(8,128)(2,1)S(1)}, bf16[6,8,128]{2,1,0:T(8,128)(2,1)}, u32[]{:S(2)}) copy-start(bf16[6,8,128]{2,1,0:T(8,128)(2,1)} %pk_ref.1) | copy-start | bytes 36868
  4.1 0.7 %copy-start.4 = (bf16[6,8,128]{2,1,0:T(8,128)(2,1)S(1)}, bf16[6,8,128]{2,1,0:T(8,128)(2,1)}, u32[]{:S(2)}) copy-start(bf16[6,8,128]{2,1,0:T(8,128)(2,1)} %pv_ref.1) | copy-start | bytes 36868
where the time goes:
time: 33.2 us; the launch traced here: 32.8 us
  Pallas kernels  27.1 us (82%)
  local copies, waits for them, and re-layouts  5.69 us (17%)
    pallas_call x1, Pallas kernels, on_device(): pl.pallas_call(functools.partial(kernel, peers), out_shape=jax.ShapeDtype...  27.1 us
    unnamed x11, local copies, waits for them, and re-layouts  5.69 us

commit v1 on v0

v1 whole, which is shorter than its diff:
```python
import functools
import math

import jax
import jax.numpy as jnp
from jax import lax
from jax.experimental import pallas as pl
from jax.experimental.pallas import tpu as pltpu
from jax.sharding import PartitionSpec as P

NEG = -1e30
F32 = jnp.float32
BF16 = jnp.bfloat16


def dot_t(a, b):
    return lax.dot_general(a, b, (((1,), (1,)), ((), ())), preferred_element_type=F32)


def dot(a, b):
    return jnp.dot(a, b, preferred_element_type=F32)


def kernel(
    peers, q_hbm, k_hbm, v_hbm, pk_hbm, pv_hbm, o_hbm,
    q_buf, k_buf, v_buf, pk_ref, pv_ref, o_buf, asked, answer, back, stat, stat_back,
    summ, top_s, total_s, acc_s,
    in_sem, out_sem, ask_send, ask_recv, back_send, back_recv, stat_sem, sum_send, sum_recv,
):
    heads, rows, width = q_buf.shape
    sums, block = pk_ref.shape[1], pk_ref.shape[2]
    blocks = rows // block
    own = blocks * sums
    gain = (width ** -0.5) * math.log2(math.e)
    spot = lax.axis_index("seq")
    slab = stat.shape[0] // 2

    k_in = pltpu.make_async_copy(k_hbm, k_buf, in_sem.at[0])
    v_in = pltpu.make_async_copy(v_hbm, v_buf, in_sem.at[1])
    q_in = pltpu.make_async_copy(q_hbm, q_buf, in_sem.at[2])
    k_in.start()
    v_in.start()
    q_in.start()
    pk_in = pltpu.make_async_copy(pk_hbm, pk_ref, in_sem.at[3])
    pv_in = pltpu.make_async_copy(pv_hbm, pv_ref, in_sem.at[4])
    pk_in.start()
    pv_in.start()

    barrier = pltpu.get_barrier_semaphore()

    def greet(i, c):
        pl.semaphore_signal(
            barrier, inc=1, device_id={"seq": i}, device_id_type=pl.DeviceIdType.MESH
        )
        return c

    lax.fori_loop(0, spot, greet, 0)

    @pl.when(spot < peers - 1)
    def _():
        greet(spot + 1, 0)

    def clear(i, c):
        summ[i] = jnp.zeros(summ.shape[1:], BF16)
        return c

    lax.fori_loop(spot + 1, summ.shape[0], clear, 0)

    @pl.when(spot == 0)
    def _():
        back[...] = jnp.zeros(back.shape, BF16)
        half = lax.broadcasted_iota(jnp.int32, stat_back.shape, 0) < slab
        stat_back[...] = jnp.where(half, NEG, 0.0)

    pl.semaphore_wait(barrier, peers - 1 - spot + jnp.where(spot > 0, 1, 0))

    def remote(src, dst, send_sem, recv_sem, to):
        return pltpu.make_async_remote_copy(
            src_ref=src,
            dst_ref=dst,
            send_sem=send_sem,
            recv_sem=recv_sem,
            device_id={"seq": to},
            device_id_type=pl.DeviceIdType.MESH,
        )

    def ask(h, to):
        src = q_hbm.at[h, pl.ds(0, block), :]
        return remote(src, asked.at[h], ask_send.at[h], ask_recv.at[h], to)

    def give(h, to):
        return remote(answer.at[h], back.at[h], back_send.at[h], back_recv.at[h], to)

    def give_stat(to):
        return remote(stat, stat_back, stat_sem.at[0], stat_sem.at[1], to)

    @pl.when(spot > 0)
    def _():
        for h in range(heads):
            ask(h, spot - 1).start()

    row_group = lax.broadcasted_iota(jnp.int32, (own, block), 0) // sums

    def summarise(which, pool_ref, buf, h):
        pool = pool_ref[h].astype(F32)
        tall = jnp.concatenate([pool] * blocks, axis=0)
        wide = jnp.concatenate(
            [jnp.where(row_group == b, tall, 0.0) for b in range(blocks)], axis=1
        ).astype(BF16)
        summ[spot, which, h] = dot(wide, buf[h]).astype(BF16)

    k_in.wait()
    pk_in.wait()
    for h in range(heads):
        summarise(0, pk_ref, k_buf, h)
    v_in.wait()
    pv_in.wait()
    for h in range(heads):
        summarise(1, pv_ref, v_buf, h)

    def sum_copy(source, to):
        return remote(summ.at[source], summ.at[source], sum_send.at[to], sum_recv.at[source], to)

    def send(i, c):
        sum_copy(spot, i).start()
        return c

    lax.fori_loop(spot + 1, peers, send, 0)
    q_in.wait()

    r = lax.broadcasted_iota(jnp.int32, (block, block), 0)
    c = lax.broadcasted_iota(jnp.int32, (block, block), 1)
    lower = c <= r

    def window(scores, v_now, v_before):
        top = jnp.max(scores, axis=1, keepdims=True)
        weights = jnp.exp2((scores - top) * gain)
        total = jnp.sum(weights, axis=1, keepdims=True)
        near = jnp.where(lower, weights, 0.0).astype(BF16)
        acc = dot(near, v_now)
        if v_before is not None:
            acc += dot(jnp.where(lower, 0.0, weights).astype(BF16), v_before)
        return top, total, acc

    def keep(h, b, top, total, acc):
        at = pl.ds(b * block, block)
        top_s[h, at, :] = jnp.broadcast_to(top, (block, width))
        total_s[h, at, :] = jnp.broadcast_to(total, (block, width))
        acc_s[h, at, :] = acc

    def near_head(h, carry):
        for b in range(blocks):
            now, before = pl.ds(b * block, block), pl.ds((b - 1) * block, block)
            q = q_buf[h, now, :]
            scores = dot_t(q, k_buf[h, now, :])
            if b:
                scores = jnp.where(lower, scores, dot_t(q, k_buf[h, before, :]))
                keep(h, b, *window(scores, v_buf[h, now, :], v_buf[h, before, :]))
            else:
                scores = jnp.where(lower, scores, NEG)
                keep(h, b, *window(scores, v_buf[h, now, :], None))
        return carry

    lax.fori_loop(0, heads // 2, near_head, 0)

    @pl.when(spot < peers - 1)
    def _():
        last = pl.ds(rows - block, block)
        lane = lax.broadcasted_iota(jnp.int32, (block, block), 1)
        stats = jnp.zeros((block, block), F32)
        for h in range(heads):
            ask(h, spot).wait_recv()
            scores = jnp.where(lower, NEG, dot_t(asked[h], k_buf[h, last, :]))
            top = jnp.max(scores, axis=1, keepdims=True)
            weights = jnp.where(lower, 0.0, jnp.exp2((scores - top) * gain))
            total = jnp.sum(weights, axis=1, keepdims=True)
            answer[h] = dot(weights.astype(BF16), v_buf[h, last, :]).astype(BF16)
            give(h, spot + 1).start()
            stats = jnp.where(lane == h, top, stats)
            stats = jnp.where(lane == slab + h, total, stats)
        stat[...] = jnp.transpose(stats)[: 2 * slab]
        give_stat(spot + 1).start()

    lax.fori_loop(heads // 2, heads, near_head, 0)

    @pl.when(spot > 0)
    def _():
        for h in range(heads):
            give(h, spot).wait_recv()
        give_stat(spot).wait_recv()

    pad = jnp.zeros((block - 2 * slab, block), F32)
    stats = jnp.transpose(jnp.concatenate([stat_back[...], pad], axis=0))
    for h in range(heads):
        at = pl.ds(0, block)
        old, new = top_s[h, at, :], stats[:, h : h + 1]
        top = jnp.maximum(old, new)
        fade, new_fade = jnp.exp2((old - top) * gain), jnp.exp2((new - top) * gain)
        top_s[h, at, :] = top
        total_s[h, at, :] = total_s[h, at, :] * fade + stats[:, slab + h : slab + h + 1] * new_fade
        acc_s[h, at, :] = acc_s[h, at, :] * fade + back[h].astype(F32) * new_fade

    def land(i, c):
        sum_copy(i, spot).wait_recv()
        return c

    lax.fori_loop(0, spot, land, 0)

    per = block // own

    def o_copy(h):
        return pltpu.make_async_copy(o_buf.at[h], o_hbm.at[h], out_sem.at[h])

    def chunk_block(h, j, b, keys, values):
        at = pl.ds(b * block, block)
        row_block = j * (block // sums) + c // sums
        scores = dot_t(q_buf[h, at, :], keys)
        scores = jnp.where(row_block < spot * blocks + b, scores, NEG)
        old = top_s[h, at, :]
        top = jnp.maximum(old, jnp.max(scores, axis=1, keepdims=True))
        weights = jnp.exp2((scores - top) * gain)
        fade = jnp.exp2((old - top) * gain)
        total = total_s[h, at, :] * fade + jnp.sum(weights, axis=1, keepdims=True)
        acc = acc_s[h, at, :] * fade + dot(weights.astype(BF16), values)
        return top, total, acc

    def far_head(h, carry):
        def rows_of(j):
            return (
                jnp.concatenate([summ[j * per + i, w, h] for i in range(per)], axis=0)
                for w in range(2)
            )

        def chunk(j, carry):
            keys, values = rows_of(j)
            for b in range(blocks):
                keep(h, b, *chunk_block(h, j, b, keys, values))
            return carry

        chunks = summ.shape[0] // per
        if chunks == 1:
            keys, values = rows_of(0)
            for b in range(blocks):
                _, total, acc = chunk_block(h, 0, b, keys, values)
                o_buf[h, pl.ds(b * block, block), :] = (acc / total).astype(BF16)
        else:
            lax.fori_loop(0, (spot * own + own - sums + block - 1) // block, chunk, 0)
            o_buf[h] = (acc_s[h] / total_s[h]).astype(BF16)
        o_copy(h).start()
        return carry

    lax.fori_loop(0, heads, far_head, 0)

    @pl.when(spot > 0)
    def _():
        for h in range(heads):
            ask(h, spot - 1).wait_send()

    @pl.when(spot < peers - 1)
    def _():
        for h in range(heads):
            give(h, spot + 1).wait_send()
        give_stat(spot + 1).wait_send()

    def sent(i, c):
        sum_copy(spot, i).wait_send()
        return c

    lax.fori_loop(spot + 1, peers, sent, 0)
    for h in range(heads):
        o_copy(h).wait()


def on_device(peers, queries, keys, values, pool_keys, pool_values):
    rows, heads, width = queries.shape
    sums, block = pool_keys.shape[1], pool_keys.shape[2]
    own = rows // block * sums
    per = block // own
    slots = -(-peers // per) * per
    q, k, v = (jnp.moveaxis(x, 1, 0) for x in (queries, keys, values))
    hbm = pl.BlockSpec(memory_space=pl.ANY)
    slab = -(-heads // 8) * 8
    out = pl.pallas_call(
        functools.partial(kernel, peers),
        out_shape=jax.ShapeDtypeStruct((heads, rows, width), BF16),
        in_specs=[hbm] * 5,
        out_specs=hbm,
        scratch_shapes=[
            pltpu.VMEM((heads, rows, width), BF16),
            pltpu.VMEM((heads, rows, width), BF16),
            pltpu.VMEM((heads, rows, width), BF16),
            pltpu.VMEM(pool_keys.shape, BF16),
            pltpu.VMEM(pool_values.shape, BF16),
            pltpu.VMEM((heads, rows, width), BF16),
            pltpu.VMEM((heads, block, width), BF16),
            pltpu.VMEM((heads, block, width), BF16),
            pltpu.VMEM((heads, block, width), BF16),
            pltpu.VMEM((2 * slab, block), F32),
            pltpu.VMEM((2 * slab, block), F32),
            pltpu.VMEM((slots, 2, heads, own, width), BF16),
            pltpu.VMEM((heads, rows, width), F32),
            pltpu.VMEM((heads, rows, width), F32),
            pltpu.VMEM((heads, rows, width), F32),
            pltpu.SemaphoreType.DMA((5,)),
            pltpu.SemaphoreType.DMA((heads,)),
            pltpu.SemaphoreType.DMA((heads,)),
            pltpu.SemaphoreType.DMA((heads,)),
            pltpu.SemaphoreType.DMA((heads,)),
            pltpu.SemaphoreType.DMA((heads,)),
            pltpu.SemaphoreType.DMA((2,)),
            pltpu.SemaphoreType.DMA((peers,)),
            pltpu.SemaphoreType.DMA((peers,)),
        ],
        compiler_params=pltpu.CompilerParams(
            collective_id=0, has_side_effects=True, vmem_limit_bytes=60 * 1024 * 1024
        ),
    )(q, k, v, pool_keys, pool_values)
    return jnp.moveaxis(out, 0, 1)


def solution(mesh):
    in_specs = (
        P(("groups", "seq"), "heads", None),
        P(("groups", "seq"), "heads", None),
        P(("groups", "seq"), "heads", None),
        P("heads", None, None),
        P("heads", None, None),
    )
    out_specs = P(("groups", "seq"), "heads", None)
    return jax.shard_map(
        functools.partial(on_device, mesh.shape["seq"]),
        mesh=mesh, in_specs=in_specs, out_specs=out_specs, check_vma=False,
    )
```

time: 33.2 us -> 26.9 us (0.81)
  the two profiles are of different devices: /device:TPU:26 before, /device:TPU:22 now
where the time goes in v1:
time: 26.9 us; the launch traced here: 26.8 us
  Pallas kernels  24.7 us (92%)
  local copies, waits for them, and re-layouts  2.06 us (8%)
    pallas_call x1, Pallas kernels, on_device(): pl.pallas_call(functools.partial(kernel, peers), out_shape=jax.ShapeDtype...  24.7 us
    unnamed x1, local copies, waits for them, and re-layouts  2.06 us

profile of v1, /device:TPU:22, one launch (start us, length us, event | category | flops | bytes accessed | tf_op | source)
XLA Modules:
  0.0 26.8 jit_solution(3257473876571815170)
XLA Ops:
  0.0 24.7 %shard_map.55 = bf16[6,512,128]{2,1,0:T(8,128)(2,1)} custom-call(bf16[6,512,128]{2,1,0:T(8,128)(2,1)} %bitcast.5, bf16[6,512,128]{2,1,0:T(8,128)(2,1)} %bitcast.6, bf16[6,512,128]{2,1,0:T(8,128)(2,1)} %bitcast.7, bf16[6,8,128]{2,1,0:T(8,128)(2,1)} %pk_hbm.1, bf16[6,8,128]{2,1,0:T(8,128)(2,1)} %pv_hbm.1), custom_call_target="tpu_custom_call" | custom-call | tf_op jit(solution)/shard_map/pallas_call | solution.py:283
  24.7 2.1 %copy.7 = bf16[512,6,128]{2,0,1:T(8,128)(2,1)} copy(bf16[512,6,128]{2,0,1:T(8,128)(2,1)} %bitcast.4) | data formatting | bytes 1572864

commit v2 on v1

--- a/solution.py
+++ b/solution.py
@@ -33,7 +33,6 @@
     own = blocks * sums
     gain = (width ** -0.5) * math.log2(math.e)
     spot = lax.axis_index("seq")
-    slab = stat.shape[0] // 2
 
     k_in = pltpu.make_async_copy(k_hbm, k_buf, in_sem.at[0])
     v_in = pltpu.make_async_copy(v_hbm, v_buf, in_sem.at[1])
@@ -61,16 +60,16 @@
         greet(spot + 1, 0)
 
     def clear(i, c):
-        summ[i] = jnp.zeros(summ.shape[1:], BF16)
+        summ[:, i] = jnp.zeros((heads,) + summ.shape[2:], BF16)
         return c
 
-    lax.fori_loop(spot + 1, summ.shape[0], clear, 0)
+    lax.fori_loop(spot + 1, summ.shape[1], clear, 0)
 
     @pl.when(spot == 0)
     def _():
         back[...] = jnp.zeros(back.shape, BF16)
-        half = lax.broadcasted_iota(jnp.int32, stat_back.shape, 0) < slab
-        stat_back[...] = jnp.where(half, NEG, 0.0)
+        top_row = lax.broadcasted_iota(jnp.int32, stat_back.shape, 1) == 0
+        stat_back[...] = jnp.where(top_row, NEG, 0.0)
 
     pl.semaphore_wait(barrier, peers - 1 - spot + jnp.where(spot > 0, 1, 0))
 
@@ -91,8 +90,8 @@
     def give(h, to):
         return remote(answer.at[h], back.at[h], back_send.at[h], back_recv.at[h], to)
 
-    def give_stat(to):
-        return remote(stat, stat_back, stat_sem.at[0], stat_sem.at[1], to)
+    def give_stat(h, to):
+        return remote(stat.at[h], stat_back.at[h], stat_sem.at[0, h], stat_sem.at[1, h], to)
 
     @pl.when(spot > 0)
     def _():
@@ -107,25 +106,26 @@
         wide = jnp.concatenate(
             [jnp.where(row_group == b, tall, 0.0) for b in range(blocks)], axis=1
         ).astype(BF16)
-        summ[spot, which, h] = dot(wide, buf[h]).astype(BF16)
+        summ[h, spot, which] = dot(wide, buf[h]).astype(BF16)
+
+    def sum_copy(h, source, to):
+        at = summ.at[h, source]
+        return remote(at, at, sum_send.at[h, to], sum_recv.at[h, source], to)
 
     k_in.wait()
     pk_in.wait()
-    for h in range(heads):
-        summarise(0, pk_ref, k_buf, h)
     v_in.wait()
     pv_in.wait()
     for h in range(heads):
+        summarise(0, pk_ref, k_buf, h)
         summarise(1, pv_ref, v_buf, h)
 
-    def sum_copy(source, to):
-        return remote(summ.at[source], summ.at[source], sum_send.at[to], sum_recv.at[source], to)
-
-    def send(i, c):
-        sum_copy(spot, i).start()
-        return c
-
-    lax.fori_loop(spot + 1, peers, send, 0)
+        def send(i, c):
+            sum_copy(h, spot, i).start()
+            return c
+
+        lax.fori_loop(spot + 1, peers, send, 0)
+
     q_in.wait()
 
     r = lax.broadcasted_iota(jnp.int32, (block, block), 0)
@@ -167,7 +167,6 @@
     def _():
         last = pl.ds(rows - block, block)
         lane = lax.broadcasted_iota(jnp.int32, (block, block), 1)
-        stats = jnp.zeros((block, block), F32)
         for h in range(heads):
             ask(h, spot).wait_recv()
             scores = jnp.where(lower, NEG, dot_t(asked[h], k_buf[h, last, :]))
@@ -176,73 +175,64 @@
             total = jnp.sum(weights, axis=1, keepdims=True)
             answer[h] = dot(weights.astype(BF16), v_buf[h, last, :]).astype(BF16)
             give(h, spot + 1).start()
-            stats = jnp.where(lane == h, top, stats)
-            stats = jnp.where(lane == slab + h, total, stats)
-        stat[...] = jnp.transpose(stats)[: 2 * slab]
-        give_stat(spot + 1).start()
+            stat[h] = jnp.transpose(jnp.where(lane == 0, top, total))[: stat.shape[1]]
+            give_stat(h, spot + 1).start()
 
     lax.fori_loop(heads // 2, heads, near_head, 0)
 
-    @pl.when(spot > 0)
-    def _():
-        for h in range(heads):
-            give(h, spot).wait_recv()
-        give_stat(spot).wait_recv()
-
-    pad = jnp.zeros((block - 2 * slab, block), F32)
-    stats = jnp.transpose(jnp.concatenate([stat_back[...], pad], axis=0))
-    for h in range(heads):
+    def merge(h):
+        pad = jnp.zeros((block - stat.shape[1], block), F32)
+        stats = jnp.transpose(jnp.concatenate([stat_back[h], pad], axis=0))
         at = pl.ds(0, block)
-        old, new = top_s[h, at, :], stats[:, h : h + 1]
+        old, new = top_s[h, at, :], stats[:, 0:1]
         top = jnp.maximum(old, new)
         fade, new_fade = jnp.exp2((old - top) * gain), jnp.exp2((new - top) * gain)
         top_s[h, at, :] = top
-        total_s[h, at, :] = total_s[h, at, :] * fade + stats[:, slab + h : slab + h + 1] * new_fade
+        total_s[h, at, :] = total_s[h, at, :] * fade + stats[:, 1:2] * new_fade
         acc_s[h, at, :] = acc_s[h, at, :] * fade + back[h].astype(F32) * new_fade
-
-    def land(i, c):
-        sum_copy(i, spot).wait_recv()
-        return c
-
-    lax.fori_loop(0, spot, land, 0)
 
     per = block // own
 
     def o_copy(h):
         return pltpu.make_async_copy(o_buf.at[h], o_hbm.at[h], out_sem.at[h])
 
-    def chunk_block(h, j, b, keys, values):
-        at = pl.ds(b * block, block)
-        row_block = j * (block // sums) + c // sums
-        scores = dot_t(q_buf[h, at, :], keys)
-        scores = jnp.where(row_block < spot * blocks + b, scores, NEG)
-        old = top_s[h, at, :]
+    key_block = lax.broadcasted_iota(jnp.int32, (rows, block), 1) // sums
+    query_block = spot * blocks + lax.broadcasted_iota(jnp.int32, (rows, block), 0) // block
+
+    def far_chunk(h, j):
+        keys, values = (
+            jnp.concatenate([summ[h, j * per + i, w] for i in range(per)], axis=0)
+            for w in range(2)
+        )
+        scores = dot_t(q_buf[h], keys)
+        scores = jnp.where(key_block + j * (block // sums) < query_block, scores, NEG)
+        old = top_s[h]
         top = jnp.maximum(old, jnp.max(scores, axis=1, keepdims=True))
         weights = jnp.exp2((scores - top) * gain)
         fade = jnp.exp2((old - top) * gain)
-        total = total_s[h, at, :] * fade + jnp.sum(weights, axis=1, keepdims=True)
-        acc = acc_s[h, at, :] * fade + dot(weights.astype(BF16), values)
-        return top, total, acc
+        total = total_s[h] * fade + jnp.sum(weights, axis=1, keepdims=True)
+        return top, total, acc_s[h] * fade + dot(weights.astype(BF16), values)
 
     def far_head(h, carry):
-        def rows_of(j):
-            return (
-                jnp.concatenate([summ[j * per + i, w, h] for i in range(per)], axis=0)
-                for w in range(2)
-            )
+        @pl.when(spot > 0)
+        def _():
+            give(h, spot).wait_recv()
+            give_stat(h, spot).wait_recv()
+
+        def land(i, c):
+            sum_copy(h, i, spot).wait_recv()
+            return c
+
+        lax.fori_loop(0, spot, land, 0)
+        merge(h)
 
         def chunk(j, carry):
-            keys, values = rows_of(j)
-            for b in range(blocks):
-                keep(h, b, *chunk_block(h, j, b, keys, values))
+            top_s[h], total_s[h], acc_s[h] = far_chunk(h, j)
             return carry
 
-        chunks = summ.shape[0] // per
-        if chunks == 1:
-            keys, values = rows_of(0)
-            for b in range(blocks):
-                _, total, acc = chunk_block(h, 0, b, keys, values)
-                o_buf[h, pl.ds(b * block, block), :] = (acc / total).astype(BF16)
+        if summ.shape[1] == per:
+            _, total, acc = far_chunk(h, 0)
+            o_buf[h] = (acc / total).astype(BF16)
         else:
             lax.fori_loop(0, (spot * own + own - sums + block - 1) // block, chunk, 0)
             o_buf[h] = (acc_s[h] / total_s[h]).astype(BF16)
@@ -260,10 +250,11 @@
     def _():
         for h in range(heads):
             give(h, spot + 1).wait_send()
-        give_stat(spot + 1).wait_send()
+            give_stat(h, spot + 1).wait_send()
 
     def sent(i, c):
-        sum_copy(spot, i).wait_send()
+        for h in range(heads):
+            sum_copy(h, spot, i).wait_send()
         return c
 
     lax.fori_loop(spot + 1, peers, sent, 0)
@@ -279,7 +270,6 @@
     slots = -(-peers // per) * per
     q, k, v = (jnp.moveaxis(x, 1, 0) for x in (queries, keys, values))
     hbm = pl.BlockSpec(memory_space=pl.ANY)
-    slab = -(-heads // 8) * 8
     out = pl.pallas_call(
         functools.partial(kernel, peers),
         out_shape=jax.ShapeDtypeStruct((heads, rows, width), BF16),
@@ -295,9 +285,9 @@
             pltpu.VMEM((heads, block, width), BF16),
             pltpu.VMEM((heads, block, width), BF16),
             pltpu.VMEM((heads, block, width), BF16),
-            pltpu.VMEM((2 * slab, block), F32),
-            pltpu.VMEM((2 * slab, block), F32),
-            pltpu.VMEM((slots, 2, heads, own, width), BF16),
+            pltpu.VMEM((heads, 8, block), F32),
+            pltpu.VMEM((heads, 8, block), F32),
+            pltpu.VMEM((heads, slots, 2, own, width), BF16),
             pltpu.VMEM((heads, rows, width), F32),
             pltpu.VMEM((heads, rows, width), F32),
             pltpu.VMEM((heads, rows, width), F32),
@@ -307,9 +297,9 @@
             pltpu.SemaphoreType.DMA((heads,)),
             pltpu.SemaphoreType.DMA((heads,)),
             pltpu.SemaphoreType.DMA((heads,)),
-            pltpu.SemaphoreType.DMA((2,)),
-            pltpu.SemaphoreType.DMA((peers,)),
-            pltpu.SemaphoreType.DMA((peers,)),
+            pltpu.SemaphoreType.DMA((2, heads)),
+            pltpu.SemaphoreType.DMA((heads, peers)),
+            pltpu.SemaphoreType.DMA((heads, peers)),
         ],
         compiler_params=pltpu.CompilerParams(
             collective_id=0, has_side_effects=True, vmem_limit_bytes=60 * 1024 * 1024

time: 26.9 us -> 22 us (0.82)
  the two profiles are of different devices: /device:TPU:22 before, /device:TPU:0 now
where the time goes in v2:
time: 22 us; the launch traced here: 21.8 us
  Pallas kernels  19.7 us (90%)
  local copies, waits for them, and re-layouts  2.06 us (9%)
    pallas_call x1, Pallas kernels, on_device(): pl.pallas_call(functools.partial(kernel, peers), out_shape=jax.ShapeDtype...  19.7 us
    unnamed x1, local copies, waits for them, and re-layouts  2.06 us

profile of v2, /device:TPU:0, one launch (start us, length us, event | category | flops | bytes accessed | tf_op | source)
XLA Modules:
  0.0 21.8 jit_solution(15013822129865662200)
XLA Ops:
  0.0 19.7 %shard_map.55 = bf16[6,512,128]{2,1,0:T(8,128)(2,1)} custom-call(bf16[6,512,128]{2,1,0:T(8,128)(2,1)} %bitcast.5, bf16[6,512,128]{2,1,0:T(8,128)(2,1)} %bitcast.6, bf16[6,512,128]{2,1,0:T(8,128)(2,1)} %bitcast.7, bf16[6,8,128]{2,1,0:T(8,128)(2,1)} %pk_hbm.1, bf16[6,8,128]{2,1,0:T(8,128)(2,1)} %pv_hbm.1), custom_call_target="tpu_custom_call" | custom-call | tf_op jit(solution)/shard_map/pallas_call | solution.py:273
  19.7 2.1 %copy.7 = bf16[512,6,128]{2,0,1:T(8,128)(2,1)} copy(bf16[512,6,128]{2,0,1:T(8,128)(2,1)} %bitcast.4) | data formatting | bytes 1572864
